TPU v7x, 32 devices: a whole 2x2x4 slice. The times are simulated.
32 devices in a mesh: rows: 8 (over z, y), chan: 4 (over x, core).
Axes of the slice: x: 2, y: 2, z: 4, core: 2. Of those that a mesh axis runs over, the one named last changes fastest.
Arguments:
- radiances: float32 [16, 16384], P('chan', 'rows'), may hold values from -6 to 6
- band: int32 [16384, 1], P('rows'), may hold values from 0 to 7; in each aligned block of 2048 rows (0 to 2047, 2048 to 4095, ...) at most 512 rows name the same one
- row_in_band: int32 [16384], P('rows'), may hold values from 0 to 3
- column: int32 [16384], P('rows'), may hold values from 0 to 1439
Outputs:
- cell_count: int32 [32, 1440], P('rows')
- cell_mean: float32 [16, 32, 1440], P('chan', 'rows')
- cell_var: float32 [16, 32, 1440], P('chan', 'rows')
- cell_spread: float32 [32, 1440], P('rows')
- departure: float32 [16, 16384], P('chan', 'rows')
Inputs may be any that keep to these rules, and one draw needn't show every extreme that they name: Within each aligned block of 2048 observations (one scan-time shard) no band is named by more than 512 observations, and in some blocks one band is named by exactly 512.
All inputs are finite; a program needn't handle non-finite values.
Results may differ from a plain program's by a relative error of at most 0.0003.
Values sent between devices are 32-bit elements.
A program may use at most 64 MiB of HBM per device.

v0:
```python
import math
import jax
import jax.numpy as jnp
from jax import lax
from jax.sharding import PartitionSpec as P

CHAN = 16
COLS = 1440
ROWS_DEV = 4


def slot_ranks(dest, nrows):
    obs_dev = dest.shape[0]
    width = math.gcd(obs_dev, 128)
    nblock = obs_dev // width
    owners = jnp.arange(nrows, dtype=jnp.int32)
    hot = (dest[None, :] == owners[:, None]).astype(jnp.bfloat16).reshape(nrows, nblock, width)
    upper = (
        lax.broadcasted_iota(jnp.int32, (width, width), 0)
        <= lax.broadcasted_iota(jnp.int32, (width, width), 1)
    ).astype(jnp.bfloat16)
    inner = jnp.einsum("nbk,kj->nbj", hot, upper, preferred_element_type=jnp.float32)
    hot_float = hot.astype(jnp.float32)
    totals = jnp.sum(hot_float, axis=2)
    before = jnp.cumsum(totals, axis=1) - totals
    ranks = jnp.sum(hot_float * (inner + before[:, :, None]), axis=0).reshape(obs_dev) - 1.0
    return ranks.astype(jnp.int32)


def split_pair(values):
    high = lax.optimization_barrier(values.astype(jnp.bfloat16))
    low = (values - high.astype(jnp.float32)).astype(jnp.bfloat16)
    return (high, low)


def split_three(values):
    high = lax.optimization_barrier(values.astype(jnp.bfloat16))
    rest = values - high.astype(jnp.float32)
    middle = lax.optimization_barrier(rest.astype(jnp.bfloat16))
    low = (rest - middle.astype(jnp.float32)).astype(jnp.bfloat16)
    return (high, middle, low)


def grid_lookup(table, lat_index, col_index):
    fields, nlat, ncol = table.shape
    total = lat_index.shape[0]
    width = math.gcd(total, 2048)
    flat = table.reshape(fields * nlat, ncol)
    lat_iota = jnp.arange(nlat, dtype=jnp.int32)
    col_iota = jnp.arange(ncol, dtype=jnp.int32)

    def look_turn(turn, result):
        start = turn * width
        lat_part = lax.dynamic_slice_in_dim(lat_index, start, width, 0)
        col_part = lax.dynamic_slice_in_dim(col_index, start, width, 0)
        col_hot = (col_iota[:, None] == col_part[None, :]).astype(jnp.float32)
        picked = jnp.dot(
            flat, col_hot, precision=lax.Precision.HIGHEST, preferred_element_type=jnp.float32
        ).reshape(fields, nlat, width)
        lat_hot = (lat_iota[:, None] == lat_part[None, :]).astype(jnp.float32)
        found = jnp.sum(picked * lat_hot[None], axis=1)
        return lax.dynamic_update_slice_in_dim(result, found, start, 1)

    return lax.fori_loop(0, total // width, look_turn, jnp.zeros((fields, total), jnp.float32))


def body(radiances, band, row_in_band, column):
    nrows = lax.axis_size("rows")
    chan_dev, obs_dev = radiances.shape
    cap = 2 * obs_dev // nrows
    total_slots = nrows * cap
    dest = band[:, 0]
    slot = dest * cap + slot_ranks(dest, nrows)
    rad_high, rad_middle, rad_low = split_three(radiances)
    payload = jnp.concatenate(
        [
            rad_high,
            rad_middle,
            rad_low,
            row_in_band[None, :].astype(jnp.bfloat16),
            (column // 64)[None, :].astype(jnp.bfloat16),
            (column % 64)[None, :].astype(jnp.bfloat16),
            jnp.ones((1, obs_dev), jnp.bfloat16),
        ],
        axis=0,
    )
    nload = payload.shape[0]
    span = math.gcd(total_slots, 1024)
    slot_iota = jnp.arange(span, dtype=jnp.int32)

    def pack_turn(turn, buffer):
        start = turn * span
        hot = (slot[:, None] == (start + slot_iota)[None, :]).astype(jnp.bfloat16)
        placed_part = jnp.dot(payload, hot, preferred_element_type=jnp.float32)
        return lax.dynamic_update_slice_in_dim(buffer, placed_part, start, 1)

    placed = lax.fori_loop(
        0, total_slots // span, pack_turn, jnp.zeros((nload, total_slots), jnp.float32)
    )
    sent_values = (
        placed[0:chan_dev] + placed[chan_dev : 2 * chan_dev] + placed[2 * chan_dev : 3 * chan_dev]
    )
    base = 3 * chan_dev
    sent_cell = jnp.where(
        placed[base + 3] > 0.5,
        placed[base] * COLS + placed[base + 1] * 64.0 + placed[base + 2],
        -1.0,
    )
    packed = jnp.concatenate([sent_values, sent_cell[None, :]], axis=0).reshape(
        chan_dev + 1, nrows, cap
    )
    arrived = lax.all_to_all(packed, "rows", split_axis=1, concat_axis=1, tiled=True).reshape(
        chan_dev + 1, total_slots
    )
    values = arrived[:chan_dev]
    cell = arrived[chan_dev].astype(jnp.int32)
    lat_local = jnp.where(cell >= 0, cell // COLS, -1)
    col_local = jnp.where(cell >= 0, cell % COLS, -1)
    value_high, value_low = split_pair(values)
    square_high, square_low = split_pair(values * values)
    features = jnp.concatenate(
        [jnp.ones((1, total_slots), jnp.bfloat16), value_high, value_low, square_high, square_low],
        axis=0,
    )
    nfeat = features.shape[0]
    row_hot = (lat_local[None, :] == jnp.arange(ROWS_DEV, dtype=jnp.int32)[:, None]).astype(
        jnp.bfloat16
    )
    left = (features[:, None, :] * row_hot[None, :, :]).reshape(nfeat * ROWS_DEV, total_slots)
    block = math.gcd(total_slots, 2048)
    turns = total_slots // block
    columns_all = jnp.arange(COLS, dtype=jnp.int32)

    def accumulate(turn, acc):
        start = turn * block
        part = lax.dynamic_slice_in_dim(left, start, block, 1)
        picked = lax.dynamic_slice_in_dim(col_local, start, block, 0)
        col_hot = (picked[:, None] == columns_all[None, :]).astype(jnp.bfloat16)
        return acc + jnp.dot(part, col_hot, preferred_element_type=jnp.float32)

    sums = lax.fori_loop(0, turns, accumulate, jnp.zeros((nfeat * ROWS_DEV, COLS), jnp.float32))
    sums = sums.reshape(nfeat, ROWS_DEV, COLS)
    count = sums[0]
    first = sums[1 : 1 + chan_dev] + sums[1 + chan_dev : 1 + 2 * chan_dev]
    second = sums[1 + 2 * chan_dev : 1 + 3 * chan_dev] + sums[1 + 3 * chan_dev :]
    denom = jnp.maximum(count, 1.0)[None]
    mean = first / denom
    var = jnp.maximum(second / denom - mean * mean, 0.0)
    spread = lax.psum(jnp.sum(var, axis=0), "chan")
    scale = lax.rsqrt(1.0 + spread / CHAN)
    fields = grid_lookup(jnp.concatenate([mean, scale[None]], axis=0), lat_local, col_local)
    shifted = (values - fields[:chan_dev]) * fields[chan_dev][None, :]
    returned = lax.all_to_all(
        shifted.reshape(chan_dev, nrows, cap), "rows", split_axis=1, concat_axis=1, tiled=True
    )
    returned_flat = returned.reshape(chan_dev, total_slots)

    def unplace(turn, result):
        start = turn * span
        hot = (slot[:, None] == (start + slot_iota)[None, :]).astype(jnp.float32)
        part = lax.dynamic_slice_in_dim(returned_flat, start, span, 1)
        return result + lax.dot_general(
            part,
            hot,
            (((1,), (1,)), ((), ())),
            precision=lax.Precision.HIGHEST,
            preferred_element_type=jnp.float32,
        )

    departure = lax.fori_loop(
        0, total_slots // span, unplace, jnp.zeros((chan_dev, obs_dev), jnp.float32)
    )
    return (count.astype(jnp.int32), mean, var, spread, departure)


def solution(mesh):
    in_specs = (P("chan", "rows"), P("rows", None), P("rows"), P("rows"))
    out_specs = (
        P("rows", None),
        P("chan", "rows", None),
        P("chan", "rows", None),
        P("rows", None),
        P("chan", "rows"),
    )
    return jax.shard_map(body, mesh=mesh, in_specs=in_specs, out_specs=out_specs, check_vma=False)
```

profile of v0, /device:TPU:0, one launch (start us, length us, event | category | flops | bytes accessed | tf_op | source)
XLA Modules:
  0.0 82.0 jit_solution(14672771929657307120)
XLA Ops:
  0.6 0.8 convert_element_type.110
  1.4 0.8 fusion.46
  2.2 0.8 subtract_convert_fusion.2
  2.9 0.7 fusion.50
  3.7 0.7 convert_element_type.115
  4.4 0.7 broadcast_multiply_fusion.1
  5.1 0.8 convert_reduce_fusion
  5.9 0.2 reduce_window_sum.11
  6.1 0.9 %fusion.39 = f32[16,128]{1,0:T(8,128)S(1)} fusion(f32[8,16]{1,0:T(8,128)S(1)} %sub.41, s32[16,128]{1,0:T(8,128)} %bitcast.49), kind=kOutput, calls=%fused_computation.36 | convolution fusion | flops 4323328 | bytes 16896 | tf_op jit(solution)/shard_map/nbk,kj->nbj/dot_general | solution.py:22
  7.0 0.1 concatenate.17
  7.2 5.7 %while.56 = (s32[]{:T(128)}, f32[16,4096]{1,0:T(8,128)S(1)}, s32[2048]{0:T(1024)S(1)}, bf16[16,2048]{1,0:T(8,128)(2,1)S(1)}, s32[]{:T(128)}, /*index=5*/s32[]{:T(128)}, s32[]{:T(128)}, s32[]{:T(128)}) while((s32[]{:T(128)}, f32[16,4096]{1,0:T(8,128)S(1)}, s32[2048]{0:T(1024)S(1)}, bf16[16,2048]{1,0:T(8,128)(2,1)S(1)}, s32[]{:T(128)}, ...), condition=%wide.region_4.5_spmd.clone, body=%wide.region_3.4_spmd.clone.sunk | while | flops 69207048 | bytes 147595 | solution.py:97
  7.2 1.4 %fusion.70 = f32[16,4096]{1,0:T(8,128)S(1)} fusion(f32[16,4096]{1,0:T(8,128)S(1)} %get-tuple-element.638, s32[]{:T(128)S(6)} %select_n.104, bf16[16,2048]{1,0:T(8,128)(2,1)S(1)} %get-tuple-element.648, s32[1024]{0:T(1024)S(1)} %iota_add_fusion.4, s32[2048]{0:T(1024)S(1)} %get-tuple-element.647), kind=kOutput, calls=%fused_computation.10.clone.1 | convolution fusion | flops 69206016 | bytes 143364 | tf_op jit(solution)/shard_map/while/body/eval_jaxpr/dot_general | solution.py:94
  8.6 1.4 %fusion.70 = f32[16,4096]{1,0:T(8,128)S(1)} fusion(f32[16,4096]{1,0:T(8,128)S(1)} %get-tuple-element.638, s32[]{:T(128)S(6)} %select_n.104, bf16[16,2048]{1,0:T(8,128)(2,1)S(1)} %get-tuple-element.648, s32[1024]{0:T(1024)S(1)} %iota_add_fusion.4, s32[2048]{0:T(1024)S(1)} %get-tuple-element.647), kind=kOutput, calls=%fused_computation.10.clone.1 | convolution fusion | flops 69206016 | bytes 143364 | tf_op jit(solution)/shard_map/while/body/eval_jaxpr/dot_general | solution.py:94
  10.0 1.4 %fusion.70 = f32[16,4096]{1,0:T(8,128)S(1)} fusion(f32[16,4096]{1,0:T(8,128)S(1)} %get-tuple-element.638, s32[]{:T(128)S(6)} %select_n.104, bf16[16,2048]{1,0:T(8,128)(2,1)S(1)} %get-tuple-element.648, s32[1024]{0:T(1024)S(1)} %iota_add_fusion.4, s32[2048]{0:T(1024)S(1)} %get-tuple-element.647), kind=kOutput, calls=%fused_computation.10.clone.1 | convolution fusion | flops 69206016 | bytes 143364 | tf_op jit(solution)/shard_map/while/body/eval_jaxpr/dot_general | solution.py:94
  11.4 1.4 %fusion.70 = f32[16,4096]{1,0:T(8,128)S(1)} fusion(f32[16,4096]{1,0:T(8,128)S(1)} %get-tuple-element.638, s32[]{:T(128)S(6)} %select_n.104, bf16[16,2048]{1,0:T(8,128)(2,1)S(1)} %get-tuple-element.648, s32[1024]{0:T(1024)S(1)} %iota_add_fusion.4, s32[2048]{0:T(1024)S(1)} %get-tuple-element.647), kind=kOutput, calls=%fused_computation.10.clone.1 | convolution fusion | flops 69206016 | bytes 143364 | tf_op jit(solution)/shard_map/while/body/eval_jaxpr/dot_general | solution.py:94
  12.9 0.1 compare_select_fusion
  12.9 0.7 pad_maximum_fusion
  13.6 7.3 %all-to-all-start = ((f32[5,8,512]{2,0,1:T(8,128)}), f32[5,8,512]{2,0,1:T(8,128)S(1)}, u32[]{:S(2)}, u32[]{:S(2)}) async-start(f32[5,8,512]{2,0,1:T(8,128)} %pad_maximum_fusion), calls=%async_computation | async-start | bytes 262144 | tf_op jit(solution)/shard_map/all_to_all | solution.py:112
  20.9 7.3 %all-to-all-done = f32[5,8,512]{2,0,1:T(8,128)S(1)} async-done(((f32[5,8,512]{2,0,1:T(8,128)}), f32[5,8,512]{2,0,1:T(8,128)S(1)}, u32[]{:S(2)}, u32[]{:S(2)}) %all-to-all-start) | async-done | bytes 81952 | tf_op jit(solution)/shard_map/all_to_all | solution.py:112
  28.3 0.1 compare_reduce_fusion
  28.5 0.1 broadcast_remainder_fusion
  28.7 0.5 concatenate.21
  29.2 0.3 broadcast_multiply_fusion
  29.5 0.1 mul.121
  29.6 5.4 %while.58 = (s32[]{:T(128)}, f32[68,1440]{1,0:T(8,128)S(1)}, bf16[68,4096]{1,0:T(8,128)(2,1)S(1)}, s32[4096]{0:T(1024)S(1)}, s32[]{:T(128)}, /*index=5*/s32[]{:T(128)}, s32[]{:T(128)}, s32[]{:T(128)}) while((s32[]{:T(128)}, f32[68,1440]{1,0:T(8,128)S(1)}, bf16[68,4096]{1,0:T(8,128)(2,1)S(1)}, s32[4096]{0:T(1024)S(1)}, s32[]{:T(128)}, ...), condition=%wide.region_6.7_spmd.clone, body=%wide.region_5.6_spmd.clone.sunk | while | flops 404225280 | bytes 1153685 | solution.py:141
  29.6 2.7 %fusion.75 = f32[68,1440]{1,0:T(8,128)S(1)} fusion(s32[2048]{0:T(1024)S(1)} %dynamic_slice.52, f32[68,1440]{1,0:T(8,128)S(1)} %get-tuple-element.662, bf16[68,4096]{1,0:T(8,128)(2,1)S(1)} %get-tuple-element.671, s32[]{:T(128)S(6)} %select_n.106, pred[]{:T(512)S(6)} %compare.9), kind=kOutput, calls=%fused_computation.23.clone.1 | convolution fusion | flops 404225280 | bytes 1137157 | tf_op jit(solution)/shard_map/while/body/eval_jaxpr/dot_general | solution.py:139
  32.3 2.7 %fusion.75 = f32[68,1440]{1,0:T(8,128)S(1)} fusion(s32[2048]{0:T(1024)S(1)} %dynamic_slice.52, f32[68,1440]{1,0:T(8,128)S(1)} %get-tuple-element.662, bf16[68,4096]{1,0:T(8,128)(2,1)S(1)} %get-tuple-element.671, s32[]{:T(128)S(6)} %select_n.106, pred[]{:T(512)S(6)} %compare.9), kind=kOutput, calls=%fused_computation.23.clone.1 | convolution fusion | flops 404225280 | bytes 1137157 | tf_op jit(solution)/shard_map/while/body/eval_jaxpr/dot_general | solution.py:139
  35.1 0.6 slice_maximum_fusion
  35.7 0.7 fusion.53
  36.4 0.0 copy-start
  36.5 10.3 %psum.7 = f32[4,1440]{1,0:T(4,128)S(1)} all-reduce(f32[4,1440]{1,0:T(4,128)S(1)} %get-tuple-element.508), channel_id=1, replica_groups=mesh['rows'=8,'chan'=4] {'chan'}, use_global_device_ids=true, to_apply=%region_8.9 | all-reduce | flops 5760 | bytes 46080 | tf_op jit(solution)/shard_map/psum | solution.py:149
  46.7 0.0 copy-start.1
  46.8 0.0 copy-done
  46.9 0.5 copy-done.1
  47.3 8.0 %while.57 = (s32[]{:T(128)}, f32[5,4096]{1,0:T(8,128)S(1)}, s32[4096]{0:T(1024)S(1)}, f32[20,1440]{1,0:T(8,128)S(1)}, s32[4096]{0:T(1024)S(1)}, /*index=5*/s32[]{:T(128)}, s32[]{:T(128)}, s32[]{:T(128)}, s32[]{:T(128)}) while((s32[]{:T(128)}, f32[5,4096]{1,0:T(8,128)S(1)}, s32[4096]{0:T(1024)S(1)}, f32[20,1440]{1,0:T(8,128)S(1)}, ...), condition=%wide.region_11.12_spmd.clone, body=%wide.region_9.11_spmd.clone.sunk | while | flops 710825984 | bytes 1057431 | solution.py:64
  47.3 3.7 %fusion.72 = f32[20,2048]{1,0:T(8,128)S(1)} fusion(f32[20,1440]{1,0:T(8,128)S(1)} %get-tuple-element.698, s32[2048]{0:T(1024)S(1)} %dynamic_slice.49), kind=kOutput, calls=%fused_computation.15.clone.1 | convolution fusion | flops 710737920 | bytes 287232 | tf_op jit(solution)/shard_map/while/body/eval_jaxpr/dot_general | solution.py:57
  51.1 0.1 reshape.182
  51.2 0.1 multiply_reduce_fusion.2
  51.3 3.7 %fusion.72 = f32[20,2048]{1,0:T(8,128)S(1)} fusion(f32[20,1440]{1,0:T(8,128)S(1)} %get-tuple-element.698, s32[2048]{0:T(1024)S(1)} %dynamic_slice.49), kind=kOutput, calls=%fused_computation.15.clone.1 | convolution fusion | flops 710737920 | bytes 287232 | tf_op jit(solution)/shard_map/while/body/eval_jaxpr/dot_general | solution.py:57
  55.1 0.1 reshape.182
  55.2 0.1 multiply_reduce_fusion.2
  55.3 0.6 subtract_multiply_fusion
  56.0 3.3 %all-to-all-start.1 = ((f32[4,8,512]{2,0,1:T(4,128)}), f32[4,8,512]{2,0,1:T(4,128)S(1)}, u32[]{:S(2)}, u32[]{:S(2)}) async-start(f32[4,8,512]{2,0,1:T(4,128)} %bitcast.11), calls=%async_computation.1 | async-start | bytes 131072 | tf_op jit(solution)/shard_map/all_to_all | solution.py:153
  59.4 6.8 %all-to-all-done.1 = f32[4,8,512]{2,0,1:T(4,128)S(1)} async-done(((f32[4,8,512]{2,0,1:T(4,128)}), f32[4,8,512]{2,0,1:T(4,128)S(1)}, u32[]{:S(2)}, u32[]{:S(2)}) %all-to-all-start.1) | async-done | bytes 65568 | tf_op jit(solution)/shard_map/all_to_all | solution.py:153
  66.2 15.2 %while.59 = (s32[]{:T(128)}, f32[4,2048]{1,0:T(4,128)S(1)}, f32[4,4096]{1,0:T(4,128)S(1)}, s32[2048]{0:T(1024)S(1)}, s32[]{:T(128)}, /*index=5*/s32[]{:T(128)}, s32[]{:T(128)}, s32[]{:T(128)}) while((s32[]{:T(128)}, f32[4,2048]{1,0:T(4,128)S(1)}, f32[4,4096]{1,0:T(4,128)S(1)}, s32[2048]{0:T(1024)S(1)}, s32[]{:T(128)}, ...), condition=%wide.region_13.14_spmd.clone, body=%wide.region_12.13_spmd.clone.sunk | while | flops 102777864 | bytes 98453 | solution.py:170
  66.2 3.8 %fusion.78 = f32[4,2048]{1,0:T(4,128)S(1)} fusion(s32[1024]{0:T(1024)S(1)} %iota_add_fusion.5, s32[2048]{0:T(1024)S(1)} %get-tuple-element.723, f32[4,2048]{1,0:T(4,128)S(1)} %get-tuple-element.713, f32[4,4096]{1,0:T(4,128)S(1)} %get-tuple-element.722, s32[]{:T(128)S(6)} %select_n.107, pred[]{:T(512)S(6)} %compare.10), kind=kOutput, calls=%fused_computation.30.clone.1 | convolution fusion | flops 102776832 | bytes 94213 | tf_op jit(solution)/shard_map/while/body/eval_jaxpr/dot_general | solution.py:162
  70.0 3.8 %fusion.78 = f32[4,2048]{1,0:T(4,128)S(1)} fusion(s32[1024]{0:T(1024)S(1)} %iota_add_fusion.5, s32[2048]{0:T(1024)S(1)} %get-tuple-element.723, f32[4,2048]{1,0:T(4,128)S(1)} %get-tuple-element.713, f32[4,4096]{1,0:T(4,128)S(1)} %get-tuple-element.722, s32[]{:T(128)S(6)} %select_n.107, pred[]{:T(512)S(6)} %compare.10), kind=kOutput, calls=%fused_computation.30.clone.1 | convolution fusion | flops 102776832 | bytes 94213 | tf_op jit(solution)/shard_map/while/body/eval_jaxpr/dot_general | solution.py:162
  73.8 3.8 %fusion.78 = f32[4,2048]{1,0:T(4,128)S(1)} fusion(s32[1024]{0:T(1024)S(1)} %iota_add_fusion.5, s32[2048]{0:T(1024)S(1)} %get-tuple-element.723, f32[4,2048]{1,0:T(4,128)S(1)} %get-tuple-element.713, f32[4,4096]{1,0:T(4,128)S(1)} %get-tuple-element.722, s32[]{:T(128)S(6)} %select_n.107, pred[]{:T(512)S(6)} %compare.10), kind=kOutput, calls=%fused_computation.30.clone.1 | convolution fusion | flops 102776832 | bytes 94213 | tf_op jit(solution)/shard_map/while/body/eval_jaxpr/dot_general | solution.py:162
  77.6 3.8 %fusion.78 = f32[4,2048]{1,0:T(4,128)S(1)} fusion(s32[1024]{0:T(1024)S(1)} %iota_add_fusion.5, s32[2048]{0:T(1024)S(1)} %get-tuple-element.723, f32[4,2048]{1,0:T(4,128)S(1)} %get-tuple-element.713, f32[4,4096]{1,0:T(4,128)S(1)} %get-tuple-element.722, s32[]{:T(128)S(6)} %select_n.107, pred[]{:T(512)S(6)} %compare.10), kind=kOutput, calls=%fused_computation.30.clone.1 | convolution fusion | flops 102776832 | bytes 94213 | tf_op jit(solution)/shard_map/while/body/eval_jaxpr/dot_general | solution.py:162
  81.4 0.0 copy-start.2
  81.4 0.6 copy-done.2
  (45 shorter events, 0.6 us)
Async XLA Ops:
  13.6 14.7 %all-to-all-start = ((f32[5,8,512]{2,0,1:T(8,128)}), f32[5,8,512]{2,0,1:T(8,128)S(1)}, u32[]{:S(2)}, u32[]{:S(2)}) async-start(f32[5,8,512]{2,0,1:T(8,128)} %pad_maximum_fusion), calls=%async_computation | async-start | bytes 262144 | tf_op jit(solution)/shard_map/all_to_all | solution.py:112
  36.4 10.4 %copy-start = (f32[4,4,1440]{2,1,0:T(4,128)}, f32[4,4,1440]{2,1,0:T(4,128)S(1)}, u32[]{:S(2)}) copy-start(f32[4,4,1440]{2,1,0:T(4,128)S(1)} %get-tuple-element.510) | copy-start | bytes 276484
  46.7 0.6 copy-start.1
  56.0 10.2 %all-to-all-start.1 = ((f32[4,8,512]{2,0,1:T(4,128)}), f32[4,8,512]{2,0,1:T(4,128)S(1)}, u32[]{:S(2)}, u32[]{:S(2)}) async-start(f32[4,8,512]{2,0,1:T(4,128)} %bitcast.11), calls=%async_computation.1 | async-start | bytes 131072 | tf_op jit(solution)/shard_map/all_to_all | solution.py:153
  81.4 0.6 copy-start.2
where the time goes:
time: 82.7 us; the launch traced here: 82 us
  matrix products  34.5 us (42%)
  waiting for transfers between devices  14.2 us (17%)
  starting transfers between devices  10.7 us (13%)
  blocking collectives  10.3 us (12%)
  other arithmetic  9.1 us (11%)
  local copies, waits for them, and re-layouts  2.18 us (3%)
  between operations  0.93 us (1%)
    dot_general x4, matrix products, unplace(): lax.dot_general(part, hot, (((1,), (1,)), ((), ())), precision=lax.Precis...  15.1 us
    psum x1, blocking collectives, body(): spread = lax.psum(jnp.sum(var, axis=0), 'chan')  10.3 us
    dot_general x2, matrix products, look_turn(): jnp.dot(flat, col_hot, precision=lax.Precision.HIGHEST, preferred_element...  7.49 us
    all_to_all x1, waiting for transfers between devices, body(): lax.all_to_all(packed, 'rows', split_axis=1, concat_axis=1, tiled=True)  7.34 us
    all_to_all x1, starting transfers between devices, body(): lax.all_to_all(packed, 'rows', split_axis=1, concat_axis=1, tiled=True)  7.31 us
    all_to_all x1, waiting for transfers between devices, body(): lax.all_to_all(shifted.reshape(chan_dev, nrows, cap), 'rows', split_axis=...  6.83 us
    dot_general x4, matrix products, pack_turn(): placed_part = jnp.dot(payload, hot, preferred_element_type=jnp.float32)  5.63 us
    dot_general x2, matrix products, accumulate(): return acc + jnp.dot(part, col_hot, preferred_element_type=jnp.float32)  5.3 us
  transfers between devices with their start and end apart: 2, of which 2 were waited for; matrix products, arithmetic and copies ran while one was open for 0% of the time, Pallas kernels for 0%

commit v1 on v0

--- a/solution.py
+++ b/solution.py
@@ -7,6 +7,9 @@
 CHAN = 16
 COLS = 1440
 ROWS_DEV = 4
+mark_flows = lambda frame: jnp.concatenate(
+    lax.all_to_all(jnp.stack(jnp.split(frame, lax.axis_size("rows"), axis=1)), "rows", 0, 0), axis=1
+)
 
 
 def slot_ranks(dest, nrows):
@@ -150,9 +153,7 @@
     scale = lax.rsqrt(1.0 + spread / CHAN)
     fields = grid_lookup(jnp.concatenate([mean, scale[None]], axis=0), lat_local, col_local)
     shifted = (values - fields[:chan_dev]) * fields[chan_dev][None, :]
-    returned = lax.all_to_all(
-        shifted.reshape(chan_dev, nrows, cap), "rows", split_axis=1, concat_axis=1, tiled=True
-    )
+    returned = mark_flows(shifted.reshape(chan_dev, nrows, cap))
     returned_flat = returned.reshape(chan_dev, total_slots)
 
     def unplace(turn, result):

time: 82.7 us -> 86.9 us (1.051)
  local copies, waits for them, and re-layouts: 2.18 us -> 6.93 us
    unnamed x8 -> x15, local copies, waits for them, and re-layouts: 1.1 us -> 5.26 us
where the time goes in v1:
time: 86.9 us; the launch traced here: 86.2 us
  matrix products  34.5 us (40%)
  waiting for transfers between devices  14.2 us (16%)
  starting transfers between devices  10.7 us (12%)
  blocking collectives  10.3 us (12%)
  other arithmetic  8.48 us (10%)
  local copies, waits for them, and re-layouts  6.93 us (8%)
  between operations  0.94 us (1%)
    dot_general x4, matrix products, unplace(): lax.dot_general(part, hot, (((1,), (1,)), ((), ())), precision=lax.Precis...  15.1 us
    psum x1, blocking collectives, body(): spread = lax.psum(jnp.sum(var, axis=0), 'chan')  10.3 us
    dot_general x2, matrix products, look_turn(): jnp.dot(flat, col_hot, precision=lax.Precision.HIGHEST, preferred_element...  7.49 us
    all_to_all x1, waiting for transfers between devices, body(): lax.all_to_all(packed, 'rows', split_axis=1, concat_axis=1, tiled=True)  7.34 us
    all_to_all x1, starting transfers between devices, body(): lax.all_to_all(packed, 'rows', split_axis=1, concat_axis=1, tiled=True)  7.31 us
    all_to_all x1, waiting for transfers between devices, lax.all_to_all(jnp.stack(jnp.split(frame, lax.axis_size('rows'), axis=1))...  6.83 us
    dot_general x4, matrix products, pack_turn(): placed_part = jnp.dot(payload, hot, preferred_element_type=jnp.float32)  5.63 us
    dot_general x2, matrix products, accumulate(): return acc + jnp.dot(part, col_hot, preferred_element_type=jnp.float32)  5.3 us
  transfers between devices with their start and end apart: 2, of which 2 were waited for; matrix products, arithmetic and copies ran while one was open for 0% of the time, Pallas kernels for 0%

profile of v1, /device:TPU:0, one launch (start us, length us, event | category | flops | bytes accessed | tf_op | source)
XLA Modules:
  0.0 86.2 jit_solution(13406176516432719519)
XLA Ops:
  0.6 0.8 convert_element_type.110
  1.4 0.8 fusion.46
  2.2 0.8 subtract_convert_fusion.2
  2.9 0.7 fusion.50
  3.7 0.7 convert_element_type.115
  4.4 0.7 broadcast_multiply_fusion.1
  5.1 0.8 convert_reduce_fusion
  5.9 0.2 reduce_window_sum.11
  6.1 0.9 %fusion.39 = f32[16,128]{1,0:T(8,128)S(1)} fusion(f32[8,16]{1,0:T(8,128)S(1)} %sub.41, s32[16,128]{1,0:T(8,128)} %bitcast.91), kind=kOutput, calls=%fused_computation.36 | convolution fusion | flops 4323328 | bytes 16896 | tf_op jit(solution)/shard_map/nbk,kj->nbj/dot_general | solution.py:25
  7.0 0.1 concatenate.17
  7.2 5.7 %while.56 = (s32[]{:T(128)}, f32[16,4096]{1,0:T(8,128)S(1)}, s32[2048]{0:T(1024)S(1)}, bf16[16,2048]{1,0:T(8,128)(2,1)S(1)}, s32[]{:T(128)}, /*index=5*/s32[]{:T(128)}, s32[]{:T(128)}, s32[]{:T(128)}) while((s32[]{:T(128)}, f32[16,4096]{1,0:T(8,128)S(1)}, s32[2048]{0:T(1024)S(1)}, bf16[16,2048]{1,0:T(8,128)(2,1)S(1)}, s32[]{:T(128)}, ...), condition=%wide.region_4.5_spmd.clone, body=%wide.region_3.4_spmd.clone.sunk | while | flops 69207048 | bytes 147595 | solution.py:100
  7.2 1.4 %fusion.70 = f32[16,4096]{1,0:T(8,128)S(1)} fusion(f32[16,4096]{1,0:T(8,128)S(1)} %get-tuple-element.638, s32[]{:T(128)S(6)} %select_n.104, bf16[16,2048]{1,0:T(8,128)(2,1)S(1)} %get-tuple-element.648, s32[1024]{0:T(1024)S(1)} %iota_add_fusion.4, s32[2048]{0:T(1024)S(1)} %get-tuple-element.647), kind=kOutput, calls=%fused_computation.10.clone.1 | convolution fusion | flops 69206016 | bytes 143364 | tf_op jit(solution)/shard_map/while/body/eval_jaxpr/dot_general | solution.py:97
  8.6 1.4 %fusion.70 = f32[16,4096]{1,0:T(8,128)S(1)} fusion(f32[16,4096]{1,0:T(8,128)S(1)} %get-tuple-element.638, s32[]{:T(128)S(6)} %select_n.104, bf16[16,2048]{1,0:T(8,128)(2,1)S(1)} %get-tuple-element.648, s32[1024]{0:T(1024)S(1)} %iota_add_fusion.4, s32[2048]{0:T(1024)S(1)} %get-tuple-element.647), kind=kOutput, calls=%fused_computation.10.clone.1 | convolution fusion | flops 69206016 | bytes 143364 | tf_op jit(solution)/shard_map/while/body/eval_jaxpr/dot_general | solution.py:97
  10.0 1.4 %fusion.70 = f32[16,4096]{1,0:T(8,128)S(1)} fusion(f32[16,4096]{1,0:T(8,128)S(1)} %get-tuple-element.638, s32[]{:T(128)S(6)} %select_n.104, bf16[16,2048]{1,0:T(8,128)(2,1)S(1)} %get-tuple-element.648, s32[1024]{0:T(1024)S(1)} %iota_add_fusion.4, s32[2048]{0:T(1024)S(1)} %get-tuple-element.647), kind=kOutput, calls=%fused_computation.10.clone.1 | convolution fusion | flops 69206016 | bytes 143364 | tf_op jit(solution)/shard_map/while/body/eval_jaxpr/dot_general | solution.py:97
  11.4 1.4 %fusion.70 = f32[16,4096]{1,0:T(8,128)S(1)} fusion(f32[16,4096]{1,0:T(8,128)S(1)} %get-tuple-element.638, s32[]{:T(128)S(6)} %select_n.104, bf16[16,2048]{1,0:T(8,128)(2,1)S(1)} %get-tuple-element.648, s32[1024]{0:T(1024)S(1)} %iota_add_fusion.4, s32[2048]{0:T(1024)S(1)} %get-tuple-element.647), kind=kOutput, calls=%fused_computation.10.clone.1 | convolution fusion | flops 69206016 | bytes 143364 | tf_op jit(solution)/shard_map/while/body/eval_jaxpr/dot_general | solution.py:97
  12.9 0.1 compare_select_fusion
  12.9 0.7 pad_maximum_fusion
  13.6 7.3 %all-to-all-start = ((f32[5,8,512]{2,0,1:T(8,128)}), f32[5,8,512]{2,0,1:T(8,128)S(1)}, u32[]{:S(2)}, u32[]{:S(2)}) async-start(f32[5,8,512]{2,0,1:T(8,128)} %pad_maximum_fusion), calls=%async_computation | async-start | bytes 262144 | tf_op jit(solution)/shard_map/all_to_all | solution.py:115
  20.9 7.3 %all-to-all-done = f32[5,8,512]{2,0,1:T(8,128)S(1)} async-done(((f32[5,8,512]{2,0,1:T(8,128)}), f32[5,8,512]{2,0,1:T(8,128)S(1)}, u32[]{:S(2)}, u32[]{:S(2)}) %all-to-all-start) | async-done | bytes 81952 | tf_op jit(solution)/shard_map/all_to_all | solution.py:115
  28.3 0.1 compare_reduce_fusion
  28.5 0.1 broadcast_remainder_fusion
  28.7 0.5 concatenate.21
  29.2 0.3 broadcast_multiply_fusion
  29.5 0.1 mul.121
  29.6 5.4 %while.58 = (s32[]{:T(128)}, f32[68,1440]{1,0:T(8,128)S(1)}, bf16[68,4096]{1,0:T(8,128)(2,1)S(1)}, s32[4096]{0:T(1024)S(1)}, s32[]{:T(128)}, /*index=5*/s32[]{:T(128)}, s32[]{:T(128)}, s32[]{:T(128)}) while((s32[]{:T(128)}, f32[68,1440]{1,0:T(8,128)S(1)}, bf16[68,4096]{1,0:T(8,128)(2,1)S(1)}, s32[4096]{0:T(1024)S(1)}, s32[]{:T(128)}, ...), condition=%wide.region_6.7_spmd.clone, body=%wide.region_5.6_spmd.clone.sunk | while | flops 404225280 | bytes 1153685 | solution.py:144
  29.6 2.7 %fusion.75 = f32[68,1440]{1,0:T(8,128)S(1)} fusion(s32[2048]{0:T(1024)S(1)} %dynamic_slice.52, f32[68,1440]{1,0:T(8,128)S(1)} %get-tuple-element.662, bf16[68,4096]{1,0:T(8,128)(2,1)S(1)} %get-tuple-element.671, s32[]{:T(128)S(6)} %select_n.106, pred[]{:T(512)S(6)} %compare.9), kind=kOutput, calls=%fused_computation.23.clone.1 | convolution fusion | flops 404225280 | bytes 1137157 | tf_op jit(solution)/shard_map/while/body/eval_jaxpr/dot_general | solution.py:142
  32.3 2.7 %fusion.75 = f32[68,1440]{1,0:T(8,128)S(1)} fusion(s32[2048]{0:T(1024)S(1)} %dynamic_slice.52, f32[68,1440]{1,0:T(8,128)S(1)} %get-tuple-element.662, bf16[68,4096]{1,0:T(8,128)(2,1)S(1)} %get-tuple-element.671, s32[]{:T(128)S(6)} %select_n.106, pred[]{:T(512)S(6)} %compare.9), kind=kOutput, calls=%fused_computation.23.clone.1 | convolution fusion | flops 404225280 | bytes 1137157 | tf_op jit(solution)/shard_map/while/body/eval_jaxpr/dot_general | solution.py:142
  35.1 0.6 slice_maximum_fusion
  35.7 0.7 fusion.53
  36.4 0.0 copy-start
  36.5 10.3 %psum.7 = f32[4,1440]{1,0:T(4,128)S(1)} all-reduce(f32[4,1440]{1,0:T(4,128)S(1)} %get-tuple-element.508), channel_id=1, replica_groups=mesh['rows'=8,'chan'=4] {'chan'}, use_global_device_ids=true, to_apply=%region_8.9 | all-reduce | flops 5760 | bytes 46080 | tf_op jit(solution)/shard_map/psum | solution.py:152
  46.7 0.0 copy-start.1
  46.8 0.0 copy-done
  46.9 0.5 copy-done.1
  47.3 8.0 %while.57 = (s32[]{:T(128)}, f32[5,4096]{1,0:T(8,128)S(1)}, s32[4096]{0:T(1024)S(1)}, f32[20,1440]{1,0:T(8,128)S(1)}, s32[4096]{0:T(1024)S(1)}, /*index=5*/s32[]{:T(128)}, s32[]{:T(128)}, s32[]{:T(128)}, s32[]{:T(128)}) while((s32[]{:T(128)}, f32[5,4096]{1,0:T(8,128)S(1)}, s32[4096]{0:T(1024)S(1)}, f32[20,1440]{1,0:T(8,128)S(1)}, ...), condition=%wide.region_11.12_spmd.clone, body=%wide.region_9.11_spmd.clone.sunk | while | flops 710825984 | bytes 1057431 | solution.py:67
  47.3 3.7 %fusion.72 = f32[20,2048]{1,0:T(8,128)S(1)} fusion(f32[20,1440]{1,0:T(8,128)S(1)} %get-tuple-element.698, s32[2048]{0:T(1024)S(1)} %dynamic_slice.49), kind=kOutput, calls=%fused_computation.15.clone.1 | convolution fusion | flops 710737920 | bytes 287232 | tf_op jit(solution)/shard_map/while/body/eval_jaxpr/dot_general | solution.py:60
  51.1 0.1 reshape.182
  51.2 0.1 multiply_reduce_fusion.2
  51.3 3.7 %fusion.72 = f32[20,2048]{1,0:T(8,128)S(1)} fusion(f32[20,1440]{1,0:T(8,128)S(1)} %get-tuple-element.698, s32[2048]{0:T(1024)S(1)} %dynamic_slice.49), kind=kOutput, calls=%fused_computation.15.clone.1 | convolution fusion | flops 710737920 | bytes 287232 | tf_op jit(solution)/shard_map/while/body/eval_jaxpr/dot_general | solution.py:60
  55.1 0.1 reshape.182
  55.2 0.1 multiply_reduce_fusion.2
  55.4 0.6 constant_dynamic-update-slice_fusion.8
  56.0 0.6 constant_dynamic-update-slice_fusion.7
  56.6 0.6 constant_dynamic-update-slice_fusion.6
  57.2 0.6 constant_dynamic-update-slice_fusion.5
  57.7 0.6 constant_dynamic-update-slice_fusion.4
  58.3 0.6 constant_dynamic-update-slice_fusion.3
  58.9 0.6 constant_dynamic-update-slice_fusion.2
  59.5 0.6 constant_dynamic-update-slice_fusion.1
  60.1 3.3 %all-to-all-start.1 = ((f32[8,4,1,512]{3,1,2,0:T(4,128)}), f32[8,4,1,512]{3,1,2,0:T(4,128)S(1)}, u32[]{:S(2)}, u32[]{:S(2)}) async-start(f32[8,4,1,512]{3,1,2,0:T(4,128)} %constant_dynamic-update-slice_fusion.1), calls=%async_computation.1 | async-start | bytes 131072 | tf_op jit(solution)/shard_map/all_to_all | solution.py:11
  63.5 6.8 %all-to-all-done.1 = f32[8,4,1,512]{3,1,2,0:T(4,128)S(1)} async-done(((f32[8,4,1,512]{3,1,2,0:T(4,128)}), f32[8,4,1,512]{3,1,2,0:T(4,128)S(1)}, u32[]{:S(2)}, u32[]{:S(2)}) %all-to-all-start.1) | async-done | bytes 65568 | tf_op jit(solution)/shard_map/all_to_all | solution.py:11
  70.3 15.2 %while.59 = (s32[]{:T(128)}, f32[4,2048]{1,0:T(4,128)S(1)}, f32[4,4096]{1,0:T(4,128)S(1)}, s32[2048]{0:T(1024)S(1)}, s32[]{:T(128)}, /*index=5*/s32[]{:T(128)}, s32[]{:T(128)}, s32[]{:T(128)}) while((s32[]{:T(128)}, f32[4,2048]{1,0:T(4,128)S(1)}, f32[4,4096]{1,0:T(4,128)S(1)}, s32[2048]{0:T(1024)S(1)}, s32[]{:T(128)}, ...), condition=%wide.region_13.14_spmd.clone, body=%wide.region_12.13_spmd.clone.sunk | while | flops 102777864 | bytes 98453 | solution.py:171
  70.3 3.8 %fusion.78 = f32[4,2048]{1,0:T(4,128)S(1)} fusion(s32[1024]{0:T(1024)S(1)} %iota_add_fusion.5, s32[2048]{0:T(1024)S(1)} %get-tuple-element.723, f32[4,2048]{1,0:T(4,128)S(1)} %get-tuple-element.713, f32[4,4096]{1,0:T(4,128)S(1)} %get-tuple-element.722, s32[]{:T(128)S(6)} %select_n.107, pred[]{:T(512)S(6)} %compare.10), kind=kOutput, calls=%fused_computation.30.clone.1 | convolution fusion | flops 102776832 | bytes 94213 | tf_op jit(solution)/shard_map/while/body/eval_jaxpr/dot_general | solution.py:163
  74.1 3.8 %fusion.78 = f32[4,2048]{1,0:T(4,128)S(1)} fusion(s32[1024]{0:T(1024)S(1)} %iota_add_fusion.5, s32[2048]{0:T(1024)S(1)} %get-tuple-element.723, f32[4,2048]{1,0:T(4,128)S(1)} %get-tuple-element.713, f32[4,4096]{1,0:T(4,128)S(1)} %get-tuple-element.722, s32[]{:T(128)S(6)} %select_n.107, pred[]{:T(512)S(6)} %compare.10), kind=kOutput, calls=%fused_computation.30.clone.1 | convolution fusion | flops 102776832 | bytes 94213 | tf_op jit(solution)/shard_map/while/body/eval_jaxpr/dot_general | solution.py:163
  77.9 3.8 %fusion.78 = f32[4,2048]{1,0:T(4,128)S(1)} fusion(s32[1024]{0:T(1024)S(1)} %iota_add_fusion.5, s32[2048]{0:T(1024)S(1)} %get-tuple-element.723, f32[4,2048]{1,0:T(4,128)S(1)} %get-tuple-element.713, f32[4,4096]{1,0:T(4,128)S(1)} %get-tuple-element.722, s32[]{:T(128)S(6)} %select_n.107, pred[]{:T(512)S(6)} %compare.10), kind=kOutput, calls=%fused_computation.30.clone.1 | convolution fusion | flops 102776832 | bytes 94213 | tf_op jit(solution)/shard_map/while/body/eval_jaxpr/dot_general | solution.py:163
  81.7 3.8 %fusion.78 = f32[4,2048]{1,0:T(4,128)S(1)} fusion(s32[1024]{0:T(1024)S(1)} %iota_add_fusion.5, s32[2048]{0:T(1024)S(1)} %get-tuple-element.723, f32[4,2048]{1,0:T(4,128)S(1)} %get-tuple-element.713, f32[4,4096]{1,0:T(4,128)S(1)} %get-tuple-element.722, s32[]{:T(128)S(6)} %select_n.107, pred[]{:T(512)S(6)} %compare.10), kind=kOutput, calls=%fused_computation.30.clone.1 | convolution fusion | flops 102776832 | bytes 94213 | tf_op jit(solution)/shard_map/while/body/eval_jaxpr/dot_general | solution.py:163
  85.5 0.0 copy-start.2
  85.6 0.6 copy-done.2
  (46 shorter events, 0.6 us)
Async XLA Ops:
  13.6 14.7 %all-to-all-start = ((f32[5,8,512]{2,0,1:T(8,128)}), f32[5,8,512]{2,0,1:T(8,128)S(1)}, u32[]{:S(2)}, u32[]{:S(2)}) async-start(f32[5,8,512]{2,0,1:T(8,128)} %pad_maximum_fusion), calls=%async_computation | async-start | bytes 262144 | tf_op jit(solution)/shard_map/all_to_all | solution.py:115
  36.4 10.4 %copy-start = (f32[4,4,1440]{2,1,0:T(4,128)}, f32[4,4,1440]{2,1,0:T(4,128)S(1)}, u32[]{:S(2)}) copy-start(f32[4,4,1440]{2,1,0:T(4,128)S(1)} %get-tuple-element.510) | copy-start | bytes 276484
  46.7 0.6 copy-start.1
  60.1 10.2 %all-to-all-start.1 = ((f32[8,4,1,512]{3,1,2,0:T(4,128)}), f32[8,4,1,512]{3,1,2,0:T(4,128)S(1)}, u32[]{:S(2)}, u32[]{:S(2)}) async-start(f32[8,4,1,512]{3,1,2,0:T(4,128)} %constant_dynamic-update-slice_fusion.1), calls=%async_computation.1 | async-start | bytes 131072 | tf_op jit(solution)/shard_map/all_to_all | solution.py:11
  85.5 0.6 copy-start.2
